TPU v7x, 32 devices: a whole 2x2x4 slice. The times are simulated.
32 devices in a mesh: seq: 4 (over z), mp: 8 (over y, x, core).
Axes of the slice: x: 2, y: 2, z: 4, core: 2. Of those that a mesh axis runs over, the one named last changes fastest.
Arguments:
- enc_rows: bfloat16 [1024, 1024], P('seq', 'mp'), may hold values from -6 to 6
- ffn_in: bfloat16 [1024, 65536], P('seq', 'mp'), may hold values from -0.1875 to 0.1875
- ffn_out: bfloat16 [65536, 1024], P('mp', 'seq'), may hold values from -0.03125 to 0.03125
- enc_gain: float32 [1024], replicated, may hold values from 0.25 to 1.75
- final_gain: float32 [1024], replicated, may hold values from 0.25 to 1.75
- sent_lengths: int32 [4, 4], replicated, may hold values from 1 to 128, 256 in all within a row
- group_table: int32 [4, 4], replicated, may hold values from 0 to 3, as said below
- dec_rows: bfloat16 [1024, 1024], P('seq', 'mp'), may hold values from -6 to 6
- dec_gain: float32 [2, 1024], replicated, may hold values from 0.25 to 1.75
- w_query: bfloat16 [2, 1024, 8192], P(None, None, 'mp'), may hold values from -0.1875 to 0.1875
- w_key: bfloat16 [2, 1024, 8192], P(None, None, 'mp'), may hold values from -0.1875 to 0.1875
- w_value: bfloat16 [2, 1024, 8192], P(None, None, 'mp'), may hold values from -0.1875 to 0.1875
- w_output: bfloat16 [2, 8192, 1024], P(None, 'mp'), may hold values from -0.0625 to 0.0625
Outputs:
- dec_out: bfloat16 [1024, 1024], P('seq', 'mp')
Inputs may be any that keep to these rules, and one draw needn't show every extreme that they name: `sent_lengths`: each row sums to 256; each row has an entry equal to 128. `group_table`: every row and every column holds each group number exactly once.
All inputs are finite; a program needn't handle non-finite values.
Results may differ from a plain program's by a relative error of at most 0.014.
Values may be sent and summed in bfloat16 or wider, within the bound.
A program may use at most 128 MiB of HBM per device.

v0:
```python
import functools

import jax
import jax.numpy as jnp
from jax import lax
from jax.experimental import pallas as pl
from jax.experimental.pallas import tpu as pltpu
from jax.sharding import PartitionSpec as P

MESH = pl.DeviceIdType.MESH

D = 1024
DH = 128
LAYERS = 2


epsilon = 1e-06


def rms_scale(values, gain_row):
    mean_square = jnp.mean(values * values, axis=-1, keepdims=True)
    return values * lax.rsqrt(mean_square + epsilon) * gain_row


def flip(index, bits):
    out = index
    for power in (1, 2, 4, 8, 16, 32):
        if bits & power:
            out = out + power - 2 * power * ((out // power) % 2)
    return out


def z_order(count):
    return sorted(range(1, count), key=lambda bits: (bits == 1, bits))


def ffn_kernel(
    n_seq,
    n_mp,
    enc_ref,
    gain_ref,
    final_gain_ref,
    lengths_ref,
    table_ref,
    dec_ref,
    dec_gain_ref,
    fin_ref,
    fout_ref,
    wq_ref,
    wk_ref,
    wv_ref,
    wo_ref,
    out_ref,
    enc_all,
    normed,
    win,
    wout,
    hidden,
    part_out,
    part_in,
    z_out,
    z_in,
    enc_zs,
    enc_zr,
    enc_ps,
    enc_pr,
    in_s,
    in_r,
    out_s,
    out_r,
    red_ps,
    red_pr,
    red_zs,
    red_zr,
    local_sem,
    wq,
    wk,
    wv,
    wo,
    w_sem,
    dec_all,
    dec_normed,
    queries,
    enc_half,
    slot_out,
    slots,
    memory,
    keys,
    values,
    attended,
    att_out,
    att_in,
    dec_ps,
    dec_pr,
    slot_zs,
    slot_zr,
    slot_ps,
    slot_pr,
    att_ps,
    att_pr,
    sel,
    mask,
    own_out_sem,
):
    s = lax.axis_index("seq")
    m = lax.axis_index("mp")
    rows, width = enc_ref.shape
    depth = fin_ref.shape[0]
    units = fin_ref.shape[1] // n_seq
    out_width = fout_ref.shape[1]
    total_rows = rows * n_seq
    per_block = out_width // width

    barrier = pltpu.get_barrier_semaphore()
    for bits in range(1, n_seq):
        pl.semaphore_signal(barrier, inc=1, device_id=(flip(s, bits), m), device_id_type=MESH)
    for bits in range(1, n_mp):
        pl.semaphore_signal(barrier, inc=1, device_id=(s, flip(m, bits)), device_id_type=MESH)
    pl.semaphore_wait(barrier, n_seq + n_mp - 2)

    my_rows = pl.ds(pl.multiple_of(s * rows, rows), rows)

    def plane_gather(buf, send_sem, recv_sem):
        def copy(slot, bits, peer):
            return pltpu.make_async_remote_copy(
                src_ref=buf.at[slot],
                dst_ref=buf.at[slot],
                send_sem=send_sem.at[bits],
                recv_sem=recv_sem.at[bits],
                device_id=(s, peer),
                device_id_type=MESH,
            )

        across = [bits for bits in range(n_mp - 2, 1, -2)]
        direct = {bits: copy(m, bits, flip(m, bits)) for bits in across + [1]}
        for bits in across + [1]:
            direct[bits].start()

        def finish():
            onward = []
            for bits in reversed(across):
                direct[bits].wait_recv()
                forward = copy(flip(m, bits), bits + 1, flip(m, 1))
                forward.start()
                onward.append(forward)
            direct[1].wait_recv()
            for forward in onward:
                forward.wait()
            for bits in across + [1]:
                direct[bits].wait_send()

        return finish

    def normalise(buf, dst, count, gain, gain_row):
        step = min(256, count)

        def body(i, carry):
            span = pl.ds(pl.multiple_of(i * step, step), step)
            squares = jnp.zeros((step, 1), jnp.float32)
            for k in range(n_mp):
                value = buf[k, span, :].astype(jnp.float32)
                squares = squares + jnp.sum(value * value, axis=1, keepdims=True)
            scale = lax.rsqrt(squares / (n_mp * width) + epsilon)
            for k in range(n_mp):
                cols = pl.ds(k * width, width)
                value = buf[k, span, :].astype(jnp.float32)
                dst[span, cols] = (value * scale * gain[pl.ds(gain_row, 1), cols]).astype(
                    jnp.bfloat16
                )
            return carry

        lax.fori_loop(0, count // step, body, 0)

    def product(left, right, layer, store):
        columns = right.shape[2]
        step = min(256, columns)

        def body(i, carry):
            cols = pl.ds(pl.multiple_of(i * step, step), step)
            store(
                cols, jnp.dot(left[...], right[layer, :, cols], preferred_element_type=jnp.float32)
            )
            return carry

        lax.fori_loop(0, columns // step, body, 0)

    def project_queries(layer):
        def store(cols, value):
            queries[:, cols] = (value * DH ** (-0.5)).astype(jnp.bfloat16)

        product(dec_normed, wq, layer, store)

    def project_memory(layer):
        def store_key(cols, value):
            keys[:, cols] = value.astype(jnp.bfloat16)

        def store_value(cols, value):
            values[:, cols] = value.astype(jnp.bfloat16)

        product(memory, wk, layer, store_key)
        product(memory, wv, layer, store_value)

    slot_rows = sel.shape[0] // n_seq
    targets = dec_ref.shape[0]
    per_sentence = targets // n_seq
    layers = wq_ref.shape[0]
    heads = wq_ref.shape[2] // DH

    def attend():
        def body(i, carry):
            span = pl.ds(pl.multiple_of(i * per_sentence, per_sentence), per_sentence)
            slot_span = pl.ds(pl.multiple_of(i * slot_rows, slot_rows), slot_rows)
            live = mask[i] > 0.5
            columns = [pl.ds(head * DH, DH) for head in range(heads)]
            scores = [
                lax.dot_general(
                    queries[span, cols],
                    keys[slot_span, cols],
                    (((1,), (1,)), ((), ())),
                    preferred_element_type=jnp.float32,
                )
                for cols in columns
            ]
            scores = [jnp.where(live, score, -jnp.inf) for score in scores]
            tops = [jnp.max(score, axis=1, keepdims=True) for score in scores]
            powers = [jnp.exp(score - top) for score, top in zip(scores, tops)]
            sums = [jnp.sum(power, axis=1, keepdims=True) for power in powers]
            weights = [(power / total).astype(jnp.bfloat16) for power, total in zip(powers, sums)]
            for cols, weight in zip(columns, weights):
                attended[span, cols] = jnp.dot(
                    weight, values[slot_span, cols], preferred_element_type=jnp.float32
                ).astype(jnp.bfloat16)
            return carry

        lax.fori_loop(0, n_seq, body, 0, unroll=n_seq <= 4)

    def att_copy(layer, slot, source):
        return pltpu.make_async_remote_copy(
            src_ref=att_out.at[layer, slot],
            dst_ref=att_in.at[layer, source],
            send_sem=att_ps.at[layer, slot],
            recv_sem=att_pr.at[layer, source],
            device_id=(s, slot),
            device_id_type=MESH,
        )

    def scatter_output(layer):
        step = max(width, 256)

        def body(i, carry):
            chip = (i + m // (step // width) + 1) % (n_mp * width // step)
            cols = pl.ds(pl.multiple_of(chip * step, step), step)
            value = jnp.dot(
                attended[...], wo[layer, :, cols], preferred_element_type=jnp.float32
            ).astype(jnp.bfloat16)
            for j in range(step // width):
                slot = chip * (step // width) + j
                att_out[layer, slot] = value[:, j * width : (j + 1) * width]

                @pl.when(slot != m)
                def _():
                    att_copy(layer, slot, m).start()

            return carry

        lax.fori_loop(0, n_mp * width // step, body, 0)

    def collect_output(layer):
        total = att_out[layer, m].astype(jnp.float32)
        for bits in range(1, n_mp):
            peer = flip(m, bits)
            att_copy(layer, peer, peer).wait_recv()
            total = total + att_in[layer, peer].astype(jnp.float32)
        for bits in range(1, n_mp):
            att_copy(layer, flip(m, bits), m).wait_send()
        return total

    own_enc = pltpu.make_async_copy(enc_ref, enc_all.at[m, my_rows], local_sem.at[0])
    own_enc.start()
    enc_z = []
    for bits in z_order(n_seq):
        copy = pltpu.make_async_remote_copy(
            src_ref=enc_ref,
            dst_ref=enc_all.at[m, my_rows],
            send_sem=enc_zs.at[bits],
            recv_sem=enc_zr.at[bits],
            device_id=(flip(s, bits), m),
            device_id_type=MESH,
        )
        copy.start()
        enc_z.append(copy)

    own_in = pltpu.make_async_copy(
        fin_ref.at[:, pl.ds(pl.multiple_of(s * units, units), units)], win.at[s], local_sem.at[1]
    )
    own_in.start()
    own_out = [
        pltpu.make_async_copy(
            fout_ref.at[
                pl.ds(pl.multiple_of(s * units, units), units), pl.ds(j * width, width)
            ],
            wout.at[s, j],
            own_out_sem.at[j],
        )
        for j in range(per_block)
    ]
    for copy in own_out:
        copy.start()
    in_copies = []
    for bits in z_order(n_seq):
        peer = flip(s, bits)
        copy = pltpu.make_async_remote_copy(
            src_ref=fin_ref.at[:, pl.ds(pl.multiple_of(peer * units, units), units)],
            dst_ref=win.at[s],
            send_sem=in_s.at[bits],
            recv_sem=in_r.at[bits],
            device_id=(peer, m),
            device_id_type=MESH,
        )
        copy.start()
        in_copies.append(copy)
    def out_copy(bits, peer, j):
        return pltpu.make_async_remote_copy(
            src_ref=fout_ref.at[
                pl.ds(pl.multiple_of(peer * units, units), units), pl.ds(j * width, width)
            ],
            dst_ref=wout.at[s, j],
            send_sem=out_s.at[bits, j],
            recv_sem=out_r.at[bits, j],
            device_id=(peer, m),
            device_id_type=MESH,
        )

    for j in range(per_block):
        out_copy(1, flip(s, 1), j).start()
    for j in range(per_block):
        for bits in range(2, n_seq):
            out_copy(bits, flip(s, bits), j).start()

    weight_copies = []
    for index, (src, dst) in enumerate(((wq_ref, wq), (wk_ref, wk), (wv_ref, wv), (wo_ref, wo))):
        copy = pltpu.make_async_copy(src, dst, w_sem.at[index])
        copy.start()
        weight_copies.append(copy)
    own_dec = pltpu.make_async_copy(dec_ref, dec_all.at[0, m], local_sem.at[3])
    own_dec.start()
    own_dec.wait()
    finish_dec = plane_gather(dec_all.at[0], dec_ps.at[0], dec_pr.at[0])

    own_enc.wait()
    for copy in enc_z:
        copy.wait()

    enc_p = []
    for bits in range(1, n_mp):
        copy = pltpu.make_async_remote_copy(
            src_ref=enc_all.at[m],
            dst_ref=enc_all.at[m],
            send_sem=enc_ps.at[bits],
            recv_sem=enc_pr.at[bits],
            device_id=(s, flip(m, bits)),
            device_id_type=MESH,
        )
        copy.start()
        enc_p.append(copy)
    for copy in enc_p:
        copy.wait()

    chunk = min(256, rows)

    normalise(enc_all, normed, total_rows, gain_ref, 0)

    for group in range(n_seq):
        start = jnp.int32(0)
        before = jnp.int32(0)
        for j in range(n_seq):
            start = start + jnp.where(table_ref[s, j] == group, before, 0)
            before = before + lengths_ref[s, j]
        position = lax.broadcasted_iota(jnp.int32, (slot_rows, rows), 0)
        column = lax.broadcasted_iota(jnp.int32, (slot_rows, rows), 1)
        wanted = jnp.minimum(position + start, rows - 1)
        sel[pl.ds(group * slot_rows, slot_rows), :] = jnp.where(wanted == column, 1.0, 0.0).astype(
            jnp.bfloat16
        )
    for source in range(n_seq):
        length = jnp.int32(0)
        for j in range(n_seq):
            length = length + jnp.where(table_ref[source, j] == s, lengths_ref[source, j], 0)
        slot = lax.broadcasted_iota(jnp.int32, (1, slot_rows), 1)
        mask[source] = jnp.where(slot < length, 1.0, 0.0)

    finish_dec()
    normalise(dec_all.at[0], dec_normed, targets, dec_gain_ref, 0)
    for copy in weight_copies:
        copy.wait()
    project_queries(0)

    own_in.wait()
    for copy in in_copies:
        copy.wait()

    tile = min(256, units)

    def hidden_chunk(i, carry):
        cols = pl.ds(pl.multiple_of((i % (units // tile)) * tile, tile), tile)
        span = pl.ds(pl.multiple_of((i // (units // tile)) * chunk, chunk), chunk)
        acc = jnp.zeros((chunk, tile), jnp.float32)
        for k in range(n_seq):
            acc = acc + jnp.dot(
                normed[span, pl.ds(k * depth, depth)],
                win[k, :, cols],
                preferred_element_type=jnp.float32,
            )
        hidden[span, cols] = jnp.maximum(acc, 0.0).astype(jnp.bfloat16)
        return carry

    lax.fori_loop(0, (total_rows // chunk) * (units // tile), hidden_chunk, 0)

    def send_copy(slot, span):
        return pltpu.make_async_remote_copy(
            src_ref=part_out.at[slot, span],
            dst_ref=part_in.at[m, span],
            send_sem=red_ps.at[slot],
            recv_sem=red_pr.at[m],
            device_id=(s, slot),
            device_id_type=MESH,
        )

    def send_block(block, j):
        slot = block * per_block + j

        def rows_chunk(i, carry):
            span = pl.ds(pl.multiple_of(i * chunk, chunk), chunk)
            part_out[slot, span, :] = jnp.dot(
                hidden[span, :], wout[block, j], preferred_element_type=jnp.float32
            ).astype(jnp.bfloat16)

            @pl.when(slot != m)
            def _():
                send_copy(slot, span).start()

            return carry

        lax.fori_loop(0, total_rows // chunk, rows_chunk, 0)

    def receive_block(bits, j):
        peer = flip_any(bits)
        out_copy(bits, peer, j).wait()
        send_block(peer, j)

    inner = (s % 2 + s // 2) % 2

    def flip_any(bits):
        if isinstance(bits, int):
            return flip(s, bits)
        return flip(s, 2) * (3 - bits) + flip(s, 3) * (bits - 2)

    later = list(range(2, n_seq))
    if n_seq == 4:
        later = [2 + inner, 3 - inner]
    for j in range(per_block):
        own_out[j].wait()
        send_block(s, j)
    for j in range(per_block):
        receive_block(1, j)
    for j in range(per_block):
        for bits in later:
            receive_block(bits, j)

    everything = pl.ds(0, total_rows)
    for bits in range(1, n_mp):
        send_copy(flip(m, bits), everything).wait_send()
    for bits in range(1, n_mp):
        peer = flip(m, bits)
        pltpu.make_async_remote_copy(
            src_ref=part_out.at[peer],
            dst_ref=part_in.at[peer],
            send_sem=red_ps.at[peer],
            recv_sem=red_pr.at[peer],
            device_id=(s, peer),
            device_id_type=MESH,
        ).wait_recv()

    def reduce_rows(block):
        span = pl.ds(pl.multiple_of(block * rows, rows), rows)
        total = part_out[m, span, :].astype(jnp.float32)
        for bits in range(1, n_mp):
            total = total + part_in[flip(m, bits), span, :].astype(jnp.float32)
        return total

    red_z = []
    for bits in z_order(n_seq):
        peer = flip(s, bits)
        z_out[bits] = reduce_rows(peer).astype(jnp.bfloat16)
        copy = pltpu.make_async_remote_copy(
            src_ref=z_out.at[bits],
            dst_ref=z_in.at[bits],
            send_sem=red_zs.at[bits],
            recv_sem=red_zr.at[bits],
            device_id=(peer, m),
            device_id_type=MESH,
        )
        copy.start()
        red_z.append(copy)
    total = reduce_rows(s)
    for bits, copy in zip(z_order(n_seq), red_z):
        copy.wait()
        total = total + z_in[bits].astype(jnp.float32)
    enc_half[...] = (enc_ref[...].astype(jnp.float32) + total).astype(jnp.bfloat16)

    def select(group):
        span = pl.ds(pl.multiple_of(group * slot_rows, slot_rows), slot_rows)
        return jnp.dot(
            sel[span, :], enc_half[...], preferred_element_type=jnp.float32
        ).astype(jnp.bfloat16)

    my_slots = pl.ds(pl.multiple_of(s * slot_rows, slot_rows), slot_rows)
    slot_z = []
    for bits in z_order(n_seq):
        peer = flip(s, bits)
        slot_out[bits] = select(peer)
        copy = pltpu.make_async_remote_copy(
            src_ref=slot_out.at[bits],
            dst_ref=slots.at[m, my_slots],
            send_sem=slot_zs.at[bits],
            recv_sem=slot_zr.at[bits],
            device_id=(peer, m),
            device_id_type=MESH,
        )
        copy.start()
        slot_z.append(copy)
    slots[m, my_slots, :] = select(s)
    for copy in slot_z:
        copy.wait()

    plane_gather(slots, slot_ps, slot_pr)()
    normalise(slots, memory, n_seq * slot_rows, final_gain_ref, 0)
    project_memory(0)

    state = dec_ref[...].astype(jnp.float32)
    for layer in range(layers):
        if layer > 0:
            dec_all[layer, m] = state.astype(jnp.bfloat16)
            plane_gather(dec_all.at[layer], dec_ps.at[layer], dec_pr.at[layer])()
            normalise(dec_all.at[layer], dec_normed, targets, dec_gain_ref, layer)
            project_queries(layer)
        attend()
        scatter_output(layer)
        if layer + 1 < layers:
            project_memory(layer + 1)
        state = state + collect_output(layer)
    out_ref[...] = state.astype(out_ref.dtype)


def whole_fast(
    enc_rows,
    ffn_in,
    ffn_out,
    enc_gain,
    final_gain,
    sent_lengths,
    group_table,
    dec_rows,
    dec_gain,
    w_query,
    w_key,
    w_value,
    w_output,
):
    n_seq, n_mp = lax.axis_size("seq"), lax.axis_size("mp")
    rows, width = enc_rows.shape
    depth, units = ffn_in.shape[0], ffn_in.shape[1] // n_seq
    out_width = ffn_out.shape[1]
    total = rows * n_seq
    full = width * n_mp
    targets = dec_rows.shape[0]
    layers, _, heads_width = w_query.shape
    slot_total = 2 * rows
    per_block = out_width // width
    half = jnp.bfloat16
    dma = pltpu.SemaphoreType.DMA
    return pl.pallas_call(
        functools.partial(ffn_kernel, n_seq, n_mp),
        out_shape=jax.ShapeDtypeStruct(dec_rows.shape, dec_rows.dtype),
        in_specs=[pl.BlockSpec(memory_space=pltpu.VMEM)] * 3
        + [pl.BlockSpec(memory_space=pltpu.SMEM)] * 2
        + [pl.BlockSpec(memory_space=pltpu.VMEM)] * 2
        + [pl.BlockSpec(memory_space=pl.ANY)] * 6,
        out_specs=pl.BlockSpec(memory_space=pltpu.VMEM),
        scratch_shapes=[
            pltpu.VMEM((n_mp, total, width), jnp.bfloat16),
            pltpu.VMEM((total, full), jnp.bfloat16),
            pltpu.VMEM((n_seq, depth, units), jnp.bfloat16),
            pltpu.VMEM((n_seq, per_block, units, width), jnp.bfloat16),
            pltpu.VMEM((total, units), jnp.bfloat16),
            pltpu.VMEM((n_mp, total, width), jnp.bfloat16),
            pltpu.VMEM((n_mp, total, width), jnp.bfloat16),
            pltpu.VMEM((n_seq, rows, width), jnp.bfloat16),
            pltpu.VMEM((n_seq, rows, width), jnp.bfloat16),
            dma((n_seq,)),
            dma((n_seq,)),
            dma((n_mp,)),
            dma((n_mp,)),
            dma((n_seq,)),
            dma((n_seq,)),
            dma((n_seq, per_block)),
            dma((n_seq, per_block)),
            dma((n_mp,)),
            dma((n_mp,)),
            dma((n_seq,)),
            dma((n_seq,)),
            dma((4,)),
            pltpu.VMEM(w_query.shape, half),
            pltpu.VMEM(w_key.shape, half),
            pltpu.VMEM(w_value.shape, half),
            pltpu.VMEM(w_output.shape, half),
            dma((4,)),
            pltpu.VMEM((layers, n_mp, targets, width), half),
            pltpu.VMEM((targets, full), half),
            pltpu.VMEM((targets, heads_width), half),
            pltpu.VMEM((rows, width), half),
            pltpu.VMEM((n_seq, slot_total // n_seq, width), half),
            pltpu.VMEM((n_mp, slot_total, width), half),
            pltpu.VMEM((slot_total, full), half),
            pltpu.VMEM((slot_total, heads_width), half),
            pltpu.VMEM((slot_total, heads_width), half),
            pltpu.VMEM((targets, heads_width), half),
            pltpu.VMEM((layers, n_mp, targets, width), half),
            pltpu.VMEM((layers, n_mp, targets, width), half),
            dma((layers, n_mp)),
            dma((layers, n_mp)),
            dma((n_seq,)),
            dma((n_seq,)),
            dma((n_mp,)),
            dma((n_mp,)),
            dma((layers, n_mp)),
            dma((layers, n_mp)),
            pltpu.VMEM((slot_total, rows), half),
            pltpu.VMEM((n_seq, 1, slot_total // n_seq), jnp.float32),
            dma((per_block,)),
        ],
        compiler_params=pltpu.CompilerParams(
            collective_id=0, has_side_effects=True, vmem_limit_bytes=60 * 1024 * 1024
        ),
    )(
        enc_rows,
        enc_gain.reshape(1, full),
        final_gain.reshape(1, full),
        sent_lengths,
        group_table,
        dec_rows,
        dec_gain,
        ffn_in,
        ffn_out,
        w_query,
        w_key,
        w_value,
        w_output,
    )


def fast_shapes(enc_rows, ffn_in, ffn_out, dec_rows, w_query):
    n_seq, n_mp = lax.axis_size("seq"), lax.axis_size("mp")
    power = (n_seq & (n_seq - 1)) == 0 and (n_mp & (n_mp - 1)) == 0
    aligned = (
        enc_rows.shape[1] % 128 == 0
        and ffn_in.shape[0] % 128 == 0
        and (ffn_in.shape[1] // n_seq) % 256 == 0
        and ffn_out.shape[1] % enc_rows.shape[1] == 0
        and enc_rows.shape[0] % 256 == 0
        and dec_rows.shape[0] % 256 == 0
        and (2 * enc_rows.shape[0] // n_seq) % 128 == 0
        and w_query.shape[2] % 256 == 0
        and w_query.shape[1] % 256 == 0
    )
    return power and aligned


def shards(
    enc_rows,
    ffn_in,
    ffn_out,
    enc_gain,
    final_gain,
    sent_lengths,
    group_table,
    dec_rows,
    dec_gain,
    w_query,
    w_key,
    w_value,
    w_output,
):
    group_count = lax.axis_size("seq")
    my_group = lax.axis_index("seq")
    col_width = enc_rows.shape[1]
    col_start = lax.axis_index("mp") * col_width
    row_count = enc_rows.shape[0]
    max_length = 2 * row_count // group_count
    fast = fast_shapes(enc_rows, ffn_in, ffn_out, dec_rows, w_query)
    if not fast:
        whole_rows = lax.all_gather(enc_rows, "mp", axis=1, tiled=True)
        normed = rms_scale(whole_rows.astype(jnp.float32), enc_gain).astype(jnp.bfloat16)
        full_in = lax.all_gather(ffn_in, "seq", axis=0, tiled=True)
        inner = jnp.dot(normed, full_in, preferred_element_type=jnp.float32)
        hidden = jnp.maximum(inner, 0.0).astype(jnp.bfloat16)
        partial_out = jnp.dot(
            hidden,
            lax.all_gather(ffn_out, "seq", axis=1, tiled=True),
            preferred_element_type=jnp.float32,
        )
    my_lengths = lax.dynamic_index_in_dim(sent_lengths, my_group, 0, keepdims=False)
    my_targets = lax.dynamic_index_in_dim(group_table, my_group, 0, keepdims=False)
    my_starts = jnp.cumsum(my_lengths) - my_lengths
    group_ids = jnp.arange(group_count, dtype=jnp.int32)
    matches = my_targets[None, :] == group_ids[:, None]
    send_starts = jnp.sum(jnp.where(matches, my_starts[None, :], 0), axis=1)
    positions = jnp.arange(max_length, dtype=jnp.int32)
    row_index = jnp.minimum(send_starts[:, None] + positions[None, :], row_count - 1)
    recv_lengths = jnp.sum(jnp.where(group_table == my_group, sent_lengths, 0), axis=1)
    live_mask = positions[None, :] < recv_lengths[:, None]
    if fast:
        return whole_fast(
            enc_rows,
            ffn_in,
            ffn_out,
            enc_gain,
            final_gain,
            sent_lengths,
            group_table,
            dec_rows,
            dec_gain,
            w_query,
            w_key,
            w_value,
            w_output,
        )
    kv_width = w_key.shape[2]
    weight_list = []
    for layer_index in range(LAYERS):
        weight_list.append(w_key[layer_index])
        weight_list.append(w_value[layer_index])
    enc_share = lax.psum_scatter(partial_out, "mp", scatter_dimension=1, tiled=True)
    encoded = enc_rows.astype(jnp.float32) + enc_share
    squares = lax.psum(jnp.sum(encoded * encoded, axis=1), "mp")
    gain_part = lax.dynamic_slice_in_dim(final_gain, col_start, col_width, 0)
    memory = (encoded * lax.rsqrt(squares / D + epsilon)[:, None] * gain_part).astype(jnp.bfloat16)
    blocks = memory[row_index]
    gathered = lax.all_gather(
        lax.all_to_all(blocks, "seq", split_axis=0, concat_axis=0, tiled=True),
        "mp",
        axis=2,
        tiled=True,
    )
    projected = tuple(
        (
            jnp.einsum(
                "std,de->ste", gathered, weight_matrix, preferred_element_type=jnp.float32
            ).astype(jnp.bfloat16)
            for weight_matrix in weight_list
        )
    )
    tgt_rows = dec_rows.shape[0]
    per_sentence = tgt_rows // group_count
    local_heads = kv_width // DH
    final_state = dec_rows.astype(jnp.float32)
    for layer_index in range(LAYERS):
        state_half = lax.all_gather(final_state.astype(jnp.bfloat16), "mp", axis=1, tiled=True)
        normed_rows = rms_scale(state_half.astype(jnp.float32), dec_gain[layer_index]).astype(
            jnp.bfloat16
        )
        queries = (
            jnp.dot(normed_rows, w_query[layer_index], preferred_element_type=jnp.float32)
            * DH ** (-0.5)
        ).astype(jnp.bfloat16)
        query_heads = queries.reshape(group_count, per_sentence, local_heads, DH)
        key_heads = projected[2 * layer_index].reshape(group_count, max_length, local_heads, DH)
        value_heads = projected[2 * layer_index + 1].reshape(
            group_count, max_length, local_heads, DH
        )
        scores = jnp.einsum(
            "sqhd,sthd->shqt", query_heads, key_heads, preferred_element_type=jnp.float32
        )
        scores = jnp.where(live_mask[:, None, None, :], scores, -jnp.inf)
        weights = jax.nn.softmax(scores, axis=-1).astype(jnp.bfloat16)
        attended = jnp.einsum(
            "shqt,sthd->sqhd", weights, value_heads, preferred_element_type=jnp.float32
        ).astype(jnp.bfloat16)
        final_state = final_state + lax.psum_scatter(
            jnp.dot(
                attended.reshape(tgt_rows, kv_width),
                w_output[layer_index],
                preferred_element_type=jnp.float32,
            ).astype(jnp.bfloat16),
            "mp",
            scatter_dimension=1,
            tiled=True,
        ).astype(jnp.float32)
    return final_state.astype(jnp.bfloat16)


def solution(mesh):
    in_specs = (
        P("seq", "mp"),
        P("seq", "mp"),
        P("mp", "seq"),
        P(),
        P(),
        P(),
        P(),
        P("seq", "mp"),
        P(),
        P(None, None, "mp"),
        P(None, None, "mp"),
        P(None, None, "mp"),
        P(None, "mp", None),
    )
    out_specs = P("seq", "mp")
    return jax.shard_map(shards, mesh=mesh, in_specs=in_specs, out_specs=out_specs, check_vma=False)
```

profile of v0, /device:TPU:0, one launch (start us, length us, event | category | flops | bytes accessed | tf_op | source)
XLA Modules:
  0.0 258.6 jit_solution(8070180594872550948)
XLA Ops:
  0.0 257.1 %shard_map.127 = bf16[256,128]{1,0:T(8,128)(2,1)} custom-call(bf16[256,128]{1,0:T(8,128)(2,1)} %enc_ref.1, f32[1,1024]{1,0:T(1,128)} %bitcast.2, f32[1,1024]{1,0:T(1,128)} %bitcast.3, s32[4,4]{1,0:T(4,128)} %lengths_ref.1, s32[4,4]{1,0:T(4,128)} %table_ref.1, bf16[256,128]{1,0:T(8,128)(2,1)} %dec_ref.1, f32[2,1024]{1,0:T(2,128)} %dec_gain_ref.1, ...), custom_call_target="tpu_custom_call" | custom-call | tf_op jit(solution)/shard_map/pallas_call | solution.py:582
  257.1 1.5 copy.15
where the time goes:
time: 260 us; the launch traced here: 259 us
  Pallas kernels  257 us (99%)
    pallas_call x1, Pallas kernels, whole_fast(): pl.pallas_call(functools.partial(ffn_kernel, n_seq, n_mp), out_shape=jax....  257 us

commit v1 on v0

--- a/solution.py
+++ b/solution.py
@@ -32,6 +32,12 @@
 
 def z_order(count):
     return sorted(range(1, count), key=lambda bits: (bits == 1, bits))
+
+
+def column_order(n_seq, per_block):
+    inner = [block * per_block + j for block in range(1, n_seq - 1) for j in range(per_block)]
+    outer = [block * per_block + j for j in range(per_block) for block in (0, n_seq - 1)]
+    return inner + outer
 
 
 def ffn_kernel(
@@ -58,8 +64,13 @@
     hidden,
     part_out,
     part_in,
-    z_out,
-    z_in,
+    tree_out,
+    tree_in,
+    late_out,
+    late_in,
+    enc_a,
+    enc_b,
+    enc_c,
     enc_zs,
     enc_zr,
     enc_ps,
@@ -68,10 +79,14 @@
     in_r,
     out_s,
     out_r,
-    red_ps,
-    red_pr,
-    red_zs,
-    red_zr,
+    rs_s,
+    rs_r,
+    tree_s,
+    tree_r,
+    late_s,
+    late_r,
+    ag_s,
+    ag_r,
     local_sem,
     wq,
     wk,
@@ -81,10 +96,9 @@
     dec_all,
     dec_normed,
     queries,
-    enc_half,
-    slot_out,
-    slots,
     memory,
+    square,
+    kv_acc,
     keys,
     values,
     attended,
@@ -92,10 +106,6 @@
     att_in,
     dec_ps,
     dec_pr,
-    slot_zs,
-    slot_zr,
-    slot_ps,
-    slot_pr,
     att_ps,
     att_pr,
     sel,
@@ -111,6 +121,9 @@
     total_rows = rows * n_seq
     per_block = out_width // width
 
+    order = column_order(n_seq, per_block)
+    early = (n_seq - 2) * per_block
+
     barrier = pltpu.get_barrier_semaphore()
     for bits in range(1, n_seq):
         pl.semaphore_signal(barrier, inc=1, device_id=(flip(s, bits), m), device_id_type=MESH)
@@ -190,17 +203,56 @@
 
         product(dec_normed, wq, layer, store)
 
+    def project_part(cols0, count, first):
+        step = min(256, wk.shape[2])
+        part = pl.ds(cols0, count)
+
+        def body(i, carry):
+            cols = pl.ds(pl.multiple_of(i * step, step), step)
+            for index, weight in enumerate((wk, wv)):
+                value = jnp.dot(
+                    memory[:, part], weight[0, part, cols], preferred_element_type=jnp.float32
+                )
+                if not first:
+                    value = value + kv_acc[index, :, cols]
+                kv_acc[index, :, cols] = value
+            return carry
+
+        lax.fori_loop(0, wk.shape[2] // step, body, 0)
+
+    def row_scale():
+        squares = jnp.sum(square[...], axis=1, keepdims=True)
+        return lax.rsqrt(squares / (n_mp * width) + epsilon)
+
+    def project_last(cols0, count):
+        step = min(256, wk.shape[2])
+        part = pl.ds(cols0, count)
+        scale = row_scale()
+
+        def body(i, carry):
+            cols = pl.ds(pl.multiple_of(i * step, step), step)
+            for index, (weight, dst) in enumerate(((wk, keys), (wv, values))):
+                value = kv_acc[index, :, cols] + jnp.dot(
+                    memory[:, part], weight[0, part, cols], preferred_element_type=jnp.float32
+                )
+                dst[:, cols] = (value * scale).astype(jnp.bfloat16)
+            return carry
+
+        lax.fori_loop(0, wk.shape[2] // step, body, 0)
+
     def project_memory(layer):
+        scale = row_scale()
+
         def store_key(cols, value):
-            keys[:, cols] = value.astype(jnp.bfloat16)
+            keys[:, cols] = (value * scale).astype(jnp.bfloat16)
 
         def store_value(cols, value):
-            values[:, cols] = value.astype(jnp.bfloat16)
+            values[:, cols] = (value * scale).astype(jnp.bfloat16)
 
         product(memory, wk, layer, store_key)
         product(memory, wv, layer, store_value)
 
-    slot_rows = sel.shape[0] // n_seq
+    slot_rows = sel.shape[1]
     targets = dec_ref.shape[0]
     per_sentence = targets // n_seq
     layers = wq_ref.shape[0]
@@ -319,29 +371,57 @@
         )
         copy.start()
         in_copies.append(copy)
-    def out_copy(bits, peer, j):
+    piece = units // 2
+
+    def out_copy(bits, j, k):
+        peer = flip_any(bits)
         return pltpu.make_async_remote_copy(
             src_ref=fout_ref.at[
-                pl.ds(pl.multiple_of(peer * units, units), units), pl.ds(j * width, width)
+                pl.ds(pl.multiple_of(peer * units + k * piece, piece), piece),
+                pl.ds(j * width, width),
             ],
-            dst_ref=wout.at[s, j],
-            send_sem=out_s.at[bits, j],
-            recv_sem=out_r.at[bits, j],
+            dst_ref=wout.at[s, j, pl.ds(k * piece, piece)],
+            send_sem=out_s.at[bits, j, k],
+            recv_sem=out_r.at[bits, j, k],
             device_id=(peer, m),
             device_id_type=MESH,
         )
 
+    inner = (s % 2 + s // 2) % 2
+
+    def flip_any(bits):
+        if isinstance(bits, int):
+            return flip(s, bits)
+        return flip(s, 2) * (3 - bits) + flip(s, 3) * (bits - 2)
+
+    def across_out(j):
+        for k in range(2):
+            for bits in (2, 3):
+                out_copy(bits, j, k).start()
+
     for j in range(per_block):
-        out_copy(1, flip(s, 1), j).start()
-    for j in range(per_block):
-        for bits in range(2, n_seq):
-            out_copy(bits, flip(s, bits), j).start()
+        for k in range(2):
+            out_copy(1, j, k).start()
+
+    @pl.when(inner == 1)
+    def _():
+        for j in range(per_block):
+            across_out(j)
 
     weight_copies = []
-    for index, (src, dst) in enumerate(((wq_ref, wq), (wk_ref, wk), (wv_ref, wv), (wo_ref, wo))):
+    for index, (src, dst) in enumerate(((wq_ref, wq), (wo_ref, wo))):
         copy = pltpu.make_async_copy(src, dst, w_sem.at[index])
         copy.start()
         weight_copies.append(copy)
+    for index, (src, dst) in enumerate(((wk_ref, wk), (wv_ref, wv))):
+        for slot, source in enumerate(order):
+            copy = pltpu.make_async_copy(
+                src.at[:, pl.ds(source * width, width)],
+                dst.at[:, pl.ds(slot * width, width)],
+                w_sem.at[2 + index * n_mp + slot],
+            )
+            copy.start()
+            weight_copies.append(copy)
     own_dec = pltpu.make_async_copy(dec_ref, dec_all.at[0, m], local_sem.at[3])
     own_dec.start()
     own_dec.wait()
@@ -351,37 +431,22 @@
     for copy in enc_z:
         copy.wait()
 
-    enc_p = []
-    for bits in range(1, n_mp):
-        copy = pltpu.make_async_remote_copy(
-            src_ref=enc_all.at[m],
-            dst_ref=enc_all.at[m],
-            send_sem=enc_ps.at[bits],
-            recv_sem=enc_pr.at[bits],
-            device_id=(s, flip(m, bits)),
-            device_id_type=MESH,
-        )
-        copy.start()
-        enc_p.append(copy)
-    for copy in enc_p:
-        copy.wait()
+    plane_gather(enc_all, enc_ps, enc_pr)()
 
     chunk = min(256, rows)
 
     normalise(enc_all, normed, total_rows, gain_ref, 0)
 
-    for group in range(n_seq):
+    for source in range(n_seq):
         start = jnp.int32(0)
         before = jnp.int32(0)
         for j in range(n_seq):
-            start = start + jnp.where(table_ref[s, j] == group, before, 0)
-            before = before + lengths_ref[s, j]
-        position = lax.broadcasted_iota(jnp.int32, (slot_rows, rows), 0)
+            start = start + jnp.where(table_ref[source, j] == s, before, 0)
+            before = before + lengths_ref[source, j]
+        slot_row = lax.broadcasted_iota(jnp.int32, (slot_rows, rows), 0)
         column = lax.broadcasted_iota(jnp.int32, (slot_rows, rows), 1)
-        wanted = jnp.minimum(position + start, rows - 1)
-        sel[pl.ds(group * slot_rows, slot_rows), :] = jnp.where(wanted == column, 1.0, 0.0).astype(
-            jnp.bfloat16
-        )
+        wanted = jnp.minimum(slot_row + start, rows - 1)
+        sel[source] = jnp.where(wanted == column, 1.0, 0.0).astype(jnp.bfloat16)
     for source in range(n_seq):
         length = jnp.int32(0)
         for j in range(n_seq):
@@ -416,126 +481,230 @@
 
     lax.fori_loop(0, (total_rows // chunk) * (units // tile), hidden_chunk, 0)
 
-    def send_copy(slot, span):
+    share = total_rows // n_mp
+    per_chunk = chunk // share
+    per_source = rows // share
+    my_share = pl.ds(pl.multiple_of(m * share, share), share)
+
+    def position(block, j):
+        within = (block % 2 + block // 2) % 2
+        outside = early + block // (n_seq - 1) + 2 * j
+        return within * ((block - 1) * per_block + j) + (1 - within) * outside
+
+    def rs_copy(p, peer, source):
         return pltpu.make_async_remote_copy(
-            src_ref=part_out.at[slot, span],
-            dst_ref=part_in.at[m, span],
-            send_sem=red_ps.at[slot],
-            recv_sem=red_pr.at[m],
-            device_id=(s, slot),
+            src_ref=part_out.at[p, pl.ds(pl.multiple_of(peer * share, share), share)],
+            dst_ref=part_in.at[p, source],
+            send_sem=rs_s.at[p, peer],
+            recv_sem=rs_r.at[p, source],
+            device_id=(s, peer),
             device_id_type=MESH,
         )
 
     def send_block(block, j):
-        slot = block * per_block + j
+        p = position(block, j)
 
         def rows_chunk(i, carry):
-            span = pl.ds(pl.multiple_of(i * chunk, chunk), chunk)
-            part_out[slot, span, :] = jnp.dot(
+            c = (i + m // per_chunk + 1) % (total_rows // chunk)
+            span = pl.ds(pl.multiple_of(c * chunk, chunk), chunk)
+            part_out[p, span, :] = jnp.dot(
                 hidden[span, :], wout[block, j], preferred_element_type=jnp.float32
             ).astype(jnp.bfloat16)
-
-            @pl.when(slot != m)
-            def _():
-                send_copy(slot, span).start()
+            for t in range(per_chunk):
+                peer = c * per_chunk + t
+
+                @pl.when(peer != m)
+                def _():
+                    rs_copy(p, peer, m).start()
 
             return carry
 
         lax.fori_loop(0, total_rows // chunk, rows_chunk, 0)
 
-    def receive_block(bits, j):
-        peer = flip_any(bits)
-        out_copy(bits, peer, j).wait()
-        send_block(peer, j)
-
-    inner = (s % 2 + s // 2) % 2
-
-    def flip_any(bits):
-        if isinstance(bits, int):
-            return flip(s, bits)
-        return flip(s, 2) * (3 - bits) + flip(s, 3) * (bits - 2)
-
-    later = list(range(2, n_seq))
-    if n_seq == 4:
-        later = [2 + inner, 3 - inner]
+    def receive_block(bits, block, j):
+        for k in range(2):
+            out_copy(bits, j, k).wait_recv()
+        send_block(block, j)
+
+    def plane_sum(p):
+        total = part_out[p, my_share, :].astype(jnp.float32)
+        for bits in range(1, n_mp):
+            peer = flip(m, bits)
+            rs_copy(p, peer, peer).wait_recv()
+            total = total + part_in[p, peer].astype(jnp.float32)
+        return total
+
+    def tree_copy(step, p0, count, peer):
+        return pltpu.make_async_remote_copy(
+            src_ref=tree_out.at[step, pl.ds(p0, count)],
+            dst_ref=tree_in.at[step, pl.ds(p0, count)],
+            send_sem=tree_s.at[step, p0],
+            recv_sem=tree_r.at[step, p0],
+            device_id=(peer, m),
+            device_id_type=MESH,
+        )
+
+    def down_copy(enc_buf, p0):
+        return pltpu.make_async_remote_copy(
+            src_ref=enc_buf.at[m],
+            dst_ref=enc_buf.at[m],
+            send_sem=tree_s.at[2, p0],
+            recv_sem=tree_r.at[2, p0],
+            device_id=(flip(s, 1), m),
+            device_id_type=MESH,
+        )
+
+    def residual(p):
+        return enc_all[order[p], my_share, :].astype(jnp.float32)
+
+    def tree_up(p0, count):
+        for p in range(p0, p0 + count):
+            tree_out[0, p] = plane_sum(p).astype(jnp.bfloat16)
+
+        @pl.when(inner == 0)
+        def _():
+            tree_copy(0, p0, count, flip(s, 1)).start()
+
+    def tree_across(p0, count):
+        @pl.when(inner == 1)
+        def _():
+            tree_copy(0, p0, count, flip(s, 1)).wait_recv()
+            for p in range(p0, p0 + count):
+                tree_out[1, p] = (
+                    tree_out[0, p].astype(jnp.float32) + tree_in[0, p].astype(jnp.float32)
+                ).astype(jnp.bfloat16)
+            tree_copy(1, p0, count, flip(s, 3)).start()
+
+    def tree_down(p0, count, enc_buf):
+        @pl.when(inner == 1)
+        def _():
+            tree_copy(1, p0, count, flip(s, 3)).wait_recv()
+            for p in range(p0, p0 + count):
+                total = tree_out[1, p].astype(jnp.float32) + tree_in[1, p].astype(jnp.float32)
+                enc_buf[m, p - p0] = (total + residual(p)).astype(jnp.bfloat16)
+            down_copy(enc_buf, p0).start()
+
+    def tree_gather(p0, enc_buf, index):
+        @pl.when(inner == 0)
+        def _():
+            down_copy(enc_buf, p0).wait_recv()
+
+        return plane_gather(enc_buf, ag_s.at[index], ag_r.at[index])
+
+    def tree_finish(p0, count, enc_buf):
+        @pl.when(inner == 0)
+        def _():
+            tree_copy(0, p0, count, flip(s, 1)).wait_send()
+
+        @pl.when(inner == 1)
+        def _():
+            tree_copy(1, p0, count, flip(s, 3)).wait_send()
+            down_copy(enc_buf, p0).wait_send()
+
+    last = early + 2
+
+    def late_copy(slot, bits):
+        return pltpu.make_async_remote_copy(
+            src_ref=late_out.at[slot],
+            dst_ref=late_in.at[slot, bits],
+            send_sem=late_s.at[slot, bits],
+            recv_sem=late_r.at[slot, bits],
+            device_id=(flip(s, bits), m),
+            device_id_type=MESH,
+        )
+
+    def late_send(slot):
+        late_out[slot] = plane_sum(last + slot).astype(jnp.bfloat16)
+        for bits in z_order(n_seq):
+            late_copy(slot, bits).start()
+
+    def late_sum():
+        for slot in range(2):
+            total = late_out[slot].astype(jnp.float32)
+            for bits in z_order(n_seq):
+                late_copy(slot, bits).wait_recv()
+                total = total + late_in[slot, bits].astype(jnp.float32)
+            enc_c[m, slot] = (total + residual(last + slot)).astype(jnp.bfloat16)
+
+    def absorb(enc_buf, p0, count):
+        for source in range(n_seq):
+            span = pl.ds(source * slot_rows, slot_rows)
+            total = jnp.zeros((slot_rows, width), jnp.float32)
+            for q in range(count):
+                block = enc_buf[pl.ds(source * per_source, per_source), q].reshape(rows, width)
+                slot = jnp.dot(sel[source], block, preferred_element_type=jnp.float32)
+                total = total + slot * slot
+                memory[span, pl.ds((p0 + q) * width, width)] = (
+                    slot * final_gain_ref[:, pl.ds(order[p0 + q] * width, width)]
+                ).astype(jnp.bfloat16)
+            if p0 == 0:
+                square[span, :] = total
+            else:
+                square[span, :] = square[span, :] + total
+
+    half = s // 2
+    near = 2 - half
+    far = 3 - 3 * half
+    near_bits = 2 + inner
+    far_bits = 3 - inner
+
     for j in range(per_block):
         own_out[j].wait()
         send_block(s, j)
     for j in range(per_block):
-        receive_block(1, j)
-    for j in range(per_block):
-        for bits in later:
-            receive_block(bits, j)
-
-    everything = pl.ds(0, total_rows)
-    for bits in range(1, n_mp):
-        send_copy(flip(m, bits), everything).wait_send()
-    for bits in range(1, n_mp):
-        peer = flip(m, bits)
-        pltpu.make_async_remote_copy(
-            src_ref=part_out.at[peer],
-            dst_ref=part_in.at[peer],
-            send_sem=red_ps.at[peer],
-            recv_sem=red_pr.at[peer],
-            device_id=(s, peer),
-            device_id_type=MESH,
-        ).wait_recv()
-
-    def reduce_rows(block):
-        span = pl.ds(pl.multiple_of(block * rows, rows), rows)
-        total = part_out[m, span, :].astype(jnp.float32)
+        receive_block(1, flip(s, 1), j)
+    late_send(half)
+    for j in range(per_block - 1):
+        receive_block(near_bits, near, j)
+    out_copy(near_bits, per_block - 1, 0).wait_recv()
+
+    @pl.when(inner == 0)
+    def _():
+        across_out(0)
+
+    out_copy(near_bits, per_block - 1, 1).wait_recv()
+    send_block(near, per_block - 1)
+    tree_up(0, early)
+
+    @pl.when(inner == 0)
+    def _():
+        for j in range(1, per_block):
+            across_out(j)
+
+    tree_across(0, early)
+    tree_down(0, early, enc_a)
+    finish_a = tree_gather(0, enc_a, 0)
+    receive_block(far_bits, far, 0)
+    finish_a()
+    tree_up(early, 2)
+    absorb(enc_a, 0, early)
+    project_part(0, early * width, True)
+    for j in range(1, per_block):
+        receive_block(far_bits, far, j)
+    tree_across(early, 2)
+    tree_down(early, 2, enc_b)
+    finish_b = tree_gather(early, enc_b, 1)
+    late_send(1 - half)
+    finish_b()
+    absorb(enc_b, early, 2)
+    project_part(early * width, 2 * width, False)
+    late_sum()
+    plane_gather(enc_c, ag_s.at[2], ag_r.at[2])()
+    absorb(enc_c, last, 2)
+    project_last(last * width, 2 * width)
+
+    for p in range(n_mp):
         for bits in range(1, n_mp):
-            total = total + part_in[flip(m, bits), span, :].astype(jnp.float32)
-        return total
-
-    red_z = []
-    for bits in z_order(n_seq):
-        peer = flip(s, bits)
-        z_out[bits] = reduce_rows(peer).astype(jnp.bfloat16)
-        copy = pltpu.make_async_remote_copy(
-            src_ref=z_out.at[bits],
-            dst_ref=z_in.at[bits],
-            send_sem=red_zs.at[bits],
-            recv_sem=red_zr.at[bits],
-            device_id=(peer, m),
-            device_id_type=MESH,
-        )
-        copy.start()
-        red_z.append(copy)
-    total = reduce_rows(s)
-    for bits, copy in zip(z_order(n_seq), red_z):
-        copy.wait()
-        total = total + z_in[bits].astype(jnp.float32)
-    enc_half[...] = (enc_ref[...].astype(jnp.float32) + total).astype(jnp.bfloat16)
-
-    def select(group):
-        span = pl.ds(pl.multiple_of(group * slot_rows, slot_rows), slot_rows)
-        return jnp.dot(
-            sel[span, :], enc_half[...], preferred_element_type=jnp.float32
-        ).astype(jnp.bfloat16)
-
-    my_slots = pl.ds(pl.multiple_of(s * slot_rows, slot_rows), slot_rows)
-    slot_z = []
-    for bits in z_order(n_seq):
-        peer = flip(s, bits)
-        slot_out[bits] = select(peer)
-        copy = pltpu.make_async_remote_copy(
-            src_ref=slot_out.at[bits],
-            dst_ref=slots.at[m, my_slots],
-            send_sem=slot_zs.at[bits],
-            recv_sem=slot_zr.at[bits],
-            device_id=(peer, m),
-            device_id_type=MESH,
-        )
-        copy.start()
-        slot_z.append(copy)
-    slots[m, my_slots, :] = select(s)
-    for copy in slot_z:
-        copy.wait()
-
-    plane_gather(slots, slot_ps, slot_pr)()
-    normalise(slots, memory, n_seq * slot_rows, final_gain_ref, 0)
-    project_memory(0)
+            rs_copy(p, flip(m, bits), m).wait_send()
+    tree_finish(0, early, enc_a)
+    tree_finish(early, 2, enc_b)
+    for slot in range(2):
+        for bits in z_order(n_seq):
+            late_copy(slot, bits).wait_send()
+    for bits in range(1, n_seq):
+        for j in range(per_block):
+            for k in range(2):
+                out_copy(bits, j, k).wait_send()
 
     state = dec_ref[...].astype(jnp.float32)
     for layer in range(layers):
@@ -577,6 +746,7 @@
     layers, _, heads_width = w_query.shape
     slot_total = 2 * rows
     per_block = out_width // width
+    share = total // n_mp
     half = jnp.bfloat16
     dma = pltpu.SemaphoreType.DMA
     return pl.pallas_call(
@@ -588,40 +758,48 @@
         + [pl.BlockSpec(memory_space=pl.ANY)] * 6,
         out_specs=pl.BlockSpec(memory_space=pltpu.VMEM),
         scratch_shapes=[
-            pltpu.VMEM((n_mp, total, width), jnp.bfloat16),
-            pltpu.VMEM((total, full), jnp.bfloat16),
-            pltpu.VMEM((n_seq, depth, units), jnp.bfloat16),
-            pltpu.VMEM((n_seq, per_block, units, width), jnp.bfloat16),
-            pltpu.VMEM((total, units), jnp.bfloat16),
-            pltpu.VMEM((n_mp, total, width), jnp.bfloat16),
-            pltpu.VMEM((n_mp, total, width), jnp.bfloat16),
-            pltpu.VMEM((n_seq, rows, width), jnp.bfloat16),
-            pltpu.VMEM((n_seq, rows, width), jnp.bfloat16),
+            pltpu.VMEM((n_mp, total, width), half),
+            pltpu.VMEM((total, full), half),
+            pltpu.VMEM((n_seq, depth, units), half),
+            pltpu.VMEM((n_seq, per_block, units, width), half),
+            pltpu.VMEM((total, units), half),
+            pltpu.VMEM((n_mp, total, width), half),
+            pltpu.VMEM((n_mp, n_mp, share, width), half),
+            pltpu.VMEM((2, n_mp, share, width), half),
+            pltpu.VMEM((2, n_mp, share, width), half),
+            pltpu.VMEM((2, share, width), half),
+            pltpu.VMEM((2, n_seq, share, width), half),
+            pltpu.VMEM((n_mp, n_mp - 4, share, width), half),
+            pltpu.VMEM((n_mp, 2, share, width), half),
+            pltpu.VMEM((n_mp, 2, share, width), half),
             dma((n_seq,)),
             dma((n_seq,)),
             dma((n_mp,)),
             dma((n_mp,)),
             dma((n_seq,)),
             dma((n_seq,)),
-            dma((n_seq, per_block)),
-            dma((n_seq, per_block)),
-            dma((n_mp,)),
-            dma((n_mp,)),
-            dma((n_seq,)),
-            dma((n_seq,)),
+            dma((n_seq, per_block, 2)),
+            dma((n_seq, per_block, 2)),
+            dma((n_mp, n_mp)),
+            dma((n_mp, n_mp)),
+            dma((3, n_mp)),
+            dma((3, n_mp)),
+            dma((2, n_seq)),
+            dma((2, n_seq)),
+            dma((3, n_mp)),
+            dma((3, n_mp)),
             dma((4,)),
             pltpu.VMEM(w_query.shape, half),
             pltpu.VMEM(w_key.shape, half),
             pltpu.VMEM(w_value.shape, half),
             pltpu.VMEM(w_output.shape, half),
-            dma((4,)),
+            dma((2 + 2 * n_mp,)),
             pltpu.VMEM((layers, n_mp, targets, width), half),
             pltpu.VMEM((targets, full), half),
             pltpu.VMEM((targets, heads_width), half),
-            pltpu.VMEM((rows, width), half),
-            pltpu.VMEM((n_seq, slot_total // n_seq, width), half),
-            pltpu.VMEM((n_mp, slot_total, width), half),
             pltpu.VMEM((slot_total, full), half),
+            pltpu.VMEM((slot_total, width), jnp.float32),
+            pltpu.VMEM((2, slot_total, heads_width), jnp.float32),
             pltpu.VMEM((slot_total, heads_width), half),
             pltpu.VMEM((slot_total, heads_width), half),
             pltpu.VMEM((targets, heads_width), half),
@@ -629,13 +807,9 @@
             pltpu.VMEM((layers, n_mp, targets, width), half),
             dma((layers, n_mp)),
             dma((layers, n_mp)),
-            dma((n_seq,)),
-            dma((n_seq,)),
-            dma((n_mp,)),
-            dma((n_mp,)),
             dma((layers, n_mp)),
             dma((layers, n_mp)),
-            pltpu.VMEM((slot_total, rows), half),
+            pltpu.VMEM((n_seq, slot_total // n_seq, rows), half),
             pltpu.VMEM((n_seq, 1, slot_total // n_seq), jnp.float32),
             dma((per_block,)),
         ],
@@ -661,7 +835,7 @@
 
 def fast_shapes(enc_rows, ffn_in, ffn_out, dec_rows, w_query):
     n_seq, n_mp = lax.axis_size("seq"), lax.axis_size("mp")
-    power = (n_seq & (n_seq - 1)) == 0 and (n_mp & (n_mp - 1)) == 0
+    power = n_seq == 4 and n_mp == 8 and ffn_out.shape[1] == 2 * enc_rows.shape[1]
     aligned = (
         enc_rows.shape[1] % 128 == 0
         and ffn_in.shape[0] % 128 == 0
@@ -711,7 +885,10 @@
         )
     my_lengths = lax.dynamic_index_in_dim(sent_lengths, my_group, 0, keepdims=False)
     my_targets = lax.dynamic_index_in_dim(group_table, my_group, 0, keepdims=False)
-    my_starts = jnp.cumsum(my_lengths) - my_lengths
+    ordinal = jnp.arange(group_count, dtype=jnp.int32)
+    my_starts = jnp.sum(
+        jnp.where(ordinal[None, :] < ordinal[:, None], my_lengths[None, :], 0), axis=1
+    )
     group_ids = jnp.arange(group_count, dtype=jnp.int32)
     matches = my_targets[None, :] == group_ids[:, None]
     send_starts = jnp.sum(jnp.where(matches, my_starts[None, :], 0), axis=1)

time: 260 us -> 275 us (1.058)
  Pallas kernels: 257 us -> 273 us
    pallas_call x1, Pallas kernels: 257 us -> 273 us  [whole_fast(): pl.pallas_call(functools.partial(ffn_kernel, n_seq, n_mp), out_shape=jax....]
where the time goes in v1:
time: 275 us
  Pallas kernels  273 us (99%)
    pallas_call x1, Pallas kernels, whole_fast(): pl.pallas_call(functools.partial(ffn_kernel, n_seq, n_mp), out_shape=jax....  273 us

profile of v1, /device:TPU:0, one launch (start us, length us, event | category | flops | bytes accessed | tf_op | source)
XLA Modules:
  0.0 274.8 jit_solution(2070488138624270252)
XLA Ops:
  0.0 273.3 %shard_map.127 = bf16[256,128]{1,0:T(8,128)(2,1)} custom-call(bf16[256,128]{1,0:T(8,128)(2,1)} %enc_ref.1, f32[1,1024]{1,0:T(1,128)} %bitcast.2, f32[1,1024]{1,0:T(1,128)} %bitcast.3, s32[4,4]{1,0:T(4,128)} %lengths_ref.1, s32[4,4]{1,0:T(4,128)} %table_ref.1, bf16[256,128]{1,0:T(8,128)(2,1)} %dec_ref.1, f32[2,1024]{1,0:T(2,128)} %dec_gain_ref.1, ...), custom_call_target="tpu_custom_call" | custom-call | tf_op jit(solution)/shard_map/pallas_call | solution.py:752
  273.3 1.5 copy.15

commit v2 on v1

--- a/solution.py
+++ b/solution.py
@@ -66,8 +66,6 @@
     part_in,
     tree_out,
     tree_in,
-    late_out,
-    late_in,
     enc_a,
     enc_b,
     enc_c,
@@ -83,8 +81,6 @@
     rs_r,
     tree_s,
     tree_r,
-    late_s,
-    late_r,
     ag_s,
     ag_r,
     local_sem,
@@ -394,10 +390,9 @@
             return flip(s, bits)
         return flip(s, 2) * (3 - bits) + flip(s, 3) * (bits - 2)
 
-    def across_out(j):
-        for k in range(2):
-            for bits in (2, 3):
-                out_copy(bits, j, k).start()
+    def across_out(j, k):
+        for bits in (3, 2):
+            out_copy(bits, j, k).start()
 
     for j in range(per_block):
         for k in range(2):
@@ -406,7 +401,8 @@
     @pl.when(inner == 1)
     def _():
         for j in range(per_block):
-            across_out(j)
+            for k in range(2):
+                across_out(j, k)
 
     weight_copies = []
     for index, (src, dst) in enumerate(((wq_ref, wq), (wo_ref, wo))):
@@ -534,23 +530,13 @@
             total = total + part_in[p, peer].astype(jnp.float32)
         return total
 
-    def tree_copy(step, p0, count, peer):
+    def tree_copy(bits, p0, count):
         return pltpu.make_async_remote_copy(
-            src_ref=tree_out.at[step, pl.ds(p0, count)],
-            dst_ref=tree_in.at[step, pl.ds(p0, count)],
-            send_sem=tree_s.at[step, p0],
-            recv_sem=tree_r.at[step, p0],
-            device_id=(peer, m),
-            device_id_type=MESH,
-        )
-
-    def down_copy(enc_buf, p0):
-        return pltpu.make_async_remote_copy(
-            src_ref=enc_buf.at[m],
-            dst_ref=enc_buf.at[m],
-            send_sem=tree_s.at[2, p0],
-            recv_sem=tree_r.at[2, p0],
-            device_id=(flip(s, 1), m),
+            src_ref=tree_out.at[min(bits, 1), pl.ds(p0, count)],
+            dst_ref=tree_in.at[min(bits, 2), pl.ds(p0, count)],
+            send_sem=tree_s.at[bits, p0],
+            recv_sem=tree_r.at[min(bits, 2), p0],
+            device_id=(flip(s, max(bits, 1)), m),
             device_id_type=MESH,
         )
 
@@ -561,70 +547,49 @@
         for p in range(p0, p0 + count):
             tree_out[0, p] = plane_sum(p).astype(jnp.bfloat16)
 
+        @pl.when(inner == 1)
+        def _():
+            tree_copy(0, p0, count).start()
+
+    def tree_across(p0, count):
         @pl.when(inner == 0)
         def _():
-            tree_copy(0, p0, count, flip(s, 1)).start()
-
-    def tree_across(p0, count):
-        @pl.when(inner == 1)
-        def _():
-            tree_copy(0, p0, count, flip(s, 1)).wait_recv()
+            tree_copy(0, p0, count).wait_recv()
             for p in range(p0, p0 + count):
                 tree_out[1, p] = (
                     tree_out[0, p].astype(jnp.float32) + tree_in[0, p].astype(jnp.float32)
                 ).astype(jnp.bfloat16)
-            tree_copy(1, p0, count, flip(s, 3)).start()
+            for bits in z_order(n_seq):
+                tree_copy(bits, p0, count).start()
 
     def tree_down(p0, count, enc_buf):
+        def combine(own):
+            for p in range(p0, p0 + count):
+                total = own[p].astype(jnp.float32) + tree_in[2, p].astype(jnp.float32)
+                enc_buf[m, p - p0] = (total + residual(p)).astype(jnp.bfloat16)
+
+        tree_copy(2, p0, count).wait_recv()
+
+        @pl.when(inner == 0)
+        def _():
+            combine(tree_out.at[1])
+
         @pl.when(inner == 1)
         def _():
-            tree_copy(1, p0, count, flip(s, 3)).wait_recv()
-            for p in range(p0, p0 + count):
-                total = tree_out[1, p].astype(jnp.float32) + tree_in[1, p].astype(jnp.float32)
-                enc_buf[m, p - p0] = (total + residual(p)).astype(jnp.bfloat16)
-            down_copy(enc_buf, p0).start()
-
-    def tree_gather(p0, enc_buf, index):
+            tree_copy(1, p0, count).wait_recv()
+            combine(tree_in.at[1])
+
+    def tree_finish(p0, count):
+        @pl.when(inner == 1)
+        def _():
+            tree_copy(0, p0, count).wait_send()
+
         @pl.when(inner == 0)
         def _():
-            down_copy(enc_buf, p0).wait_recv()
-
-        return plane_gather(enc_buf, ag_s.at[index], ag_r.at[index])
-
-    def tree_finish(p0, count, enc_buf):
-        @pl.when(inner == 0)
-        def _():
-            tree_copy(0, p0, count, flip(s, 1)).wait_send()
-
-        @pl.when(inner == 1)
-        def _():
-            tree_copy(1, p0, count, flip(s, 3)).wait_send()
-            down_copy(enc_buf, p0).wait_send()
+            for bits in z_order(n_seq):
+                tree_copy(bits, p0, count).wait_send()
 
     last = early + 2
-
-    def late_copy(slot, bits):
-        return pltpu.make_async_remote_copy(
-            src_ref=late_out.at[slot],
-            dst_ref=late_in.at[slot, bits],
-            send_sem=late_s.at[slot, bits],
-            recv_sem=late_r.at[slot, bits],
-            device_id=(flip(s, bits), m),
-            device_id_type=MESH,
-        )
-
-    def late_send(slot):
-        late_out[slot] = plane_sum(last + slot).astype(jnp.bfloat16)
-        for bits in z_order(n_seq):
-            late_copy(slot, bits).start()
-
-    def late_sum():
-        for slot in range(2):
-            total = late_out[slot].astype(jnp.float32)
-            for bits in z_order(n_seq):
-                late_copy(slot, bits).wait_recv()
-                total = total + late_in[slot, bits].astype(jnp.float32)
-            enc_c[m, slot] = (total + residual(last + slot)).astype(jnp.bfloat16)
 
     def absorb(enc_buf, p0, count):
         for source in range(n_seq):
@@ -642,53 +607,73 @@
             else:
                 square[span, :] = square[span, :] + total
 
-    half = s // 2
-    near = 2 - half
-    far = 3 - 3 * half
+    last = early + 2
+    near = 2 - s // 2
+    far = 3 - 3 * (s // 2)
     near_bits = 2 + inner
-    far_bits = 3 - inner
 
     for j in range(per_block):
         own_out[j].wait()
         send_block(s, j)
     for j in range(per_block):
         receive_block(1, flip(s, 1), j)
-    late_send(half)
     for j in range(per_block - 1):
         receive_block(near_bits, near, j)
     out_copy(near_bits, per_block - 1, 0).wait_recv()
 
     @pl.when(inner == 0)
     def _():
-        across_out(0)
+        out_copy(2, 0, 0).start()
 
     out_copy(near_bits, per_block - 1, 1).wait_recv()
+
+    @pl.when(inner == 0)
+    def _():
+        out_copy(2, 0, 1).start()
+        for k in range(2):
+            out_copy(2, 1, k).start()
+
     send_block(near, per_block - 1)
     tree_up(0, early)
+    tree_across(0, early)
 
     @pl.when(inner == 0)
     def _():
-        for j in range(1, per_block):
-            across_out(j)
-
-    tree_across(0, early)
+        for j in range(per_block):
+            for k in range(2):
+                out_copy(3, j, k).start()
+
+    @pl.when(inner == 1)
+    def _():
+        receive_block(2, far, 0)
+        tree_up(early, 2)
+        receive_block(2, far, 1)
+        tree_up(last, 2)
+
     tree_down(0, early, enc_a)
-    finish_a = tree_gather(0, enc_a, 0)
-    receive_block(far_bits, far, 0)
-    finish_a()
-    tree_up(early, 2)
+    plane_gather(enc_a, ag_s.at[0], ag_r.at[0])()
     absorb(enc_a, 0, early)
     project_part(0, early * width, True)
-    for j in range(1, per_block):
-        receive_block(far_bits, far, j)
-    tree_across(early, 2)
+
+    @pl.when(inner == 0)
+    def _():
+        receive_block(3, far, 0)
+        tree_up(early, 2)
+        tree_across(early, 2)
+        receive_block(3, far, 1)
+
     tree_down(early, 2, enc_b)
-    finish_b = tree_gather(early, enc_b, 1)
-    late_send(1 - half)
+    finish_b = plane_gather(enc_b, ag_s.at[1], ag_r.at[1])
+
+    @pl.when(inner == 0)
+    def _():
+        tree_up(last, 2)
+        tree_across(last, 2)
+
     finish_b()
     absorb(enc_b, early, 2)
     project_part(early * width, 2 * width, False)
-    late_sum()
+    tree_down(last, 2, enc_c)
     plane_gather(enc_c, ag_s.at[2], ag_r.at[2])()
     absorb(enc_c, last, 2)
     project_last(last * width, 2 * width)
@@ -696,11 +681,9 @@
     for p in range(n_mp):
         for bits in range(1, n_mp):
             rs_copy(p, flip(m, bits), m).wait_send()
-    tree_finish(0, early, enc_a)
-    tree_finish(early, 2, enc_b)
-    for slot in range(2):
-        for bits in z_order(n_seq):
-            late_copy(slot, bits).wait_send()
+    tree_finish(0, early)
+    tree_finish(early, 2)
+    tree_finish(last, 2)
     for bits in range(1, n_seq):
         for j in range(per_block):
             for k in range(2):
@@ -766,9 +749,7 @@
             pltpu.VMEM((n_mp, total, width), half),
             pltpu.VMEM((n_mp, n_mp, share, width), half),
             pltpu.VMEM((2, n_mp, share, width), half),
-            pltpu.VMEM((2, n_mp, share, width), half),
-            pltpu.VMEM((2, share, width), half),
-            pltpu.VMEM((2, n_seq, share, width), half),
+            pltpu.VMEM((3, n_mp, share, width), half),
             pltpu.VMEM((n_mp, n_mp - 4, share, width), half),
             pltpu.VMEM((n_mp, 2, share, width), half),
             pltpu.VMEM((n_mp, 2, share, width), half),
@@ -782,10 +763,8 @@
             dma((n_seq, per_block, 2)),
             dma((n_mp, n_mp)),
             dma((n_mp, n_mp)),
+            dma((4, n_mp)),
             dma((3, n_mp)),
-            dma((3, n_mp)),
-            dma((2, n_seq)),
-            dma((2, n_seq)),
             dma((3, n_mp)),
             dma((3, n_mp)),
             dma((4,)),

time: 275 us -> 258 us (0.938)
  Pallas kernels: 273 us -> 256 us
    pallas_call x1, Pallas kernels: 273 us -> 256 us  [whole_fast(): pl.pallas_call(functools.partial(ffn_kernel, n_seq, n_mp), out_shape=jax....]
where the time goes in v2:
time: 258 us; the launch traced here: 257 us
  Pallas kernels  256 us (99%)
    pallas_call x1, Pallas kernels, whole_fast(): pl.pallas_call(functools.partial(ffn_kernel, n_seq, n_mp), out_shape=jax....  256 us

profile of v2, /device:TPU:0, one launch (start us, length us, event | category | flops | bytes accessed | tf_op | source)
XLA Modules:
  0.0 257.1 jit_solution(14565756037973830614)
XLA Ops:
  0.0 255.7 %shard_map.127 = bf16[256,128]{1,0:T(8,128)(2,1)} custom-call(bf16[256,128]{1,0:T(8,128)(2,1)} %enc_ref.1, f32[1,1024]{1,0:T(1,128)} %bitcast.2, f32[1,1024]{1,0:T(1,128)} %bitcast.3, s32[4,4]{1,0:T(4,128)} %lengths_ref.1, s32[4,4]{1,0:T(4,128)} %table_ref.1, bf16[256,128]{1,0:T(8,128)(2,1)} %dec_ref.1, f32[2,1024]{1,0:T(2,128)} %dec_gain_ref.1, ...), custom_call_target="tpu_custom_call" | custom-call | tf_op jit(solution)/shard_map/pallas_call | solution.py:735
  255.7 1.5 copy.15

commit v3 on v2

--- a/solution.py
+++ b/solution.py
@@ -90,6 +90,7 @@
     wo,
     w_sem,
     dec_all,
+    dec_next,
     dec_normed,
     queries,
     memory,
@@ -193,11 +194,11 @@
 
         lax.fori_loop(0, columns // step, body, 0)
 
-    def project_queries(layer):
+    def project_queries(layer, span):
         def store(cols, value):
-            queries[:, cols] = (value * DH ** (-0.5)).astype(jnp.bfloat16)
-
-        product(dec_normed, wq, layer, store)
+            queries[span, cols] = (value * DH ** (-0.5)).astype(jnp.bfloat16)
+
+        product(dec_normed.at[span], wq, layer, store)
 
     def project_part(cols0, count, first):
         step = min(256, wk.shape[2])
@@ -254,7 +255,7 @@
     layers = wq_ref.shape[0]
     heads = wq_ref.shape[2] // DH
 
-    def attend():
+    def attend(first, count):
         def body(i, carry):
             span = pl.ds(pl.multiple_of(i * per_sentence, per_sentence), per_sentence)
             slot_span = pl.ds(pl.multiple_of(i * slot_rows, slot_rows), slot_rows)
@@ -280,54 +281,58 @@
                 ).astype(jnp.bfloat16)
             return carry
 
-        lax.fori_loop(0, n_seq, body, 0, unroll=n_seq <= 4)
-
-    def att_copy(layer, slot, source):
+        lax.fori_loop(first, first + count, body, 0, unroll=True)
+
+    parts = 2
+    part_rows = targets // parts
+
+    def rows_of(part):
+        return pl.ds(part * part_rows, part_rows)
+
+    def att_copy(layer, part, slot, source):
         return pltpu.make_async_remote_copy(
-            src_ref=att_out.at[layer, slot],
-            dst_ref=att_in.at[layer, source],
-            send_sem=att_ps.at[layer, slot],
-            recv_sem=att_pr.at[layer, source],
+            src_ref=att_out.at[layer, part, slot],
+            dst_ref=att_in.at[layer, part, source],
+            send_sem=att_ps.at[layer, part, slot],
+            recv_sem=att_pr.at[layer, part, source],
             device_id=(s, slot),
             device_id_type=MESH,
         )
 
-    def scatter_output(layer):
+    def scatter_output(layer, part):
         step = max(width, 256)
 
         def body(i, carry):
             chip = (i + m // (step // width) + 1) % (n_mp * width // step)
             cols = pl.ds(pl.multiple_of(chip * step, step), step)
             value = jnp.dot(
-                attended[...], wo[layer, :, cols], preferred_element_type=jnp.float32
+                attended[rows_of(part), :], wo[layer, :, cols], preferred_element_type=jnp.float32
             ).astype(jnp.bfloat16)
             for j in range(step // width):
                 slot = chip * (step // width) + j
-                att_out[layer, slot] = value[:, j * width : (j + 1) * width]
+                att_out[layer, part, slot] = value[:, j * width : (j + 1) * width]
 
                 @pl.when(slot != m)
                 def _():
-                    att_copy(layer, slot, m).start()
+                    att_copy(layer, part, slot, m).start()
 
             return carry
 
         lax.fori_loop(0, n_mp * width // step, body, 0)
 
-    def collect_output(layer):
-        total = att_out[layer, m].astype(jnp.float32)
+    def collect_output(layer, part):
+        total = att_out[layer, part, m].astype(jnp.float32)
         for bits in range(1, n_mp):
             peer = flip(m, bits)
-            att_copy(layer, peer, peer).wait_recv()
-            total = total + att_in[layer, peer].astype(jnp.float32)
-        for bits in range(1, n_mp):
-            att_copy(layer, flip(m, bits), m).wait_send()
+            att_copy(layer, part, peer, peer).wait_recv()
+            total = total + att_in[layer, part, peer].astype(jnp.float32)
         return total
 
     own_enc = pltpu.make_async_copy(enc_ref, enc_all.at[m, my_rows], local_sem.at[0])
     own_enc.start()
-    enc_z = []
-    for bits in z_order(n_seq):
-        copy = pltpu.make_async_remote_copy(
+
+    def enc_copy(bits):
+        return pltpu.make_async_remote_copy(
             src_ref=enc_ref,
             dst_ref=enc_all.at[m, my_rows],
             send_sem=enc_zs.at[bits],
@@ -335,8 +340,19 @@
             device_id=(flip(s, bits), m),
             device_id_type=MESH,
         )
-        copy.start()
-        enc_z.append(copy)
+
+    for bits in (2, 1):
+        enc_copy(bits).start()
+    across_rows = pl.ds(pl.multiple_of(flip(s, 2) * rows, rows), rows)
+    enc_onward = pltpu.make_async_remote_copy(
+        src_ref=enc_all.at[m, across_rows],
+        dst_ref=enc_all.at[m, across_rows],
+        send_sem=enc_zs.at[3],
+        recv_sem=enc_zr.at[3],
+        device_id=(flip(s, 1), m),
+        device_id_type=MESH,
+    )
+    inner = (s % 2 + s // 2) % 2
 
     own_in = pltpu.make_async_copy(
         fin_ref.at[:, pl.ds(pl.multiple_of(s * units, units), units)], win.at[s], local_sem.at[1]
@@ -354,10 +370,9 @@
     ]
     for copy in own_out:
         copy.start()
-    in_copies = []
-    for bits in z_order(n_seq):
+    def in_copy(bits):
         peer = flip(s, bits)
-        copy = pltpu.make_async_remote_copy(
+        return pltpu.make_async_remote_copy(
             src_ref=fin_ref.at[:, pl.ds(pl.multiple_of(peer * units, units), units)],
             dst_ref=win.at[s],
             send_sem=in_s.at[bits],
@@ -365,8 +380,21 @@
             device_id=(peer, m),
             device_id_type=MESH,
         )
-        copy.start()
-        in_copies.append(copy)
+
+    @pl.when(inner == 1)
+    def _():
+        for bits in (2, 3):
+            in_copy(bits).start()
+
+    enc_copy(2).wait_recv()
+    enc_onward.start()
+
+    @pl.when(inner == 0)
+    def _():
+        for bits in (2, 3):
+            in_copy(bits).start()
+
+    in_copy(1).start()
     piece = units // 2
 
     def out_copy(bits, j, k):
@@ -382,8 +410,6 @@
             device_id=(peer, m),
             device_id_type=MESH,
         )
-
-    inner = (s % 2 + s // 2) % 2
 
     def flip_any(bits):
         if isinstance(bits, int):
@@ -418,14 +444,17 @@
             )
             copy.start()
             weight_copies.append(copy)
-    own_dec = pltpu.make_async_copy(dec_ref, dec_all.at[0, m], local_sem.at[3])
+    own_dec = pltpu.make_async_copy(dec_ref, dec_all.at[m], local_sem.at[3])
     own_dec.start()
     own_dec.wait()
-    finish_dec = plane_gather(dec_all.at[0], dec_ps.at[0], dec_pr.at[0])
+    finish_dec = plane_gather(dec_all, dec_ps.at[0], dec_pr.at[0])
 
     own_enc.wait()
-    for copy in enc_z:
-        copy.wait()
+    enc_copy(1).wait_recv()
+    enc_onward.wait_recv()
+    for bits in (2, 1):
+        enc_copy(bits).wait_send()
+    enc_onward.wait_send()
 
     plane_gather(enc_all, enc_ps, enc_pr)()
 
@@ -451,14 +480,14 @@
         mask[source] = jnp.where(slot < length, 1.0, 0.0)
 
     finish_dec()
-    normalise(dec_all.at[0], dec_normed, targets, dec_gain_ref, 0)
+    normalise(dec_all, dec_normed, targets, dec_gain_ref, 0)
     for copy in weight_copies:
         copy.wait()
-    project_queries(0)
+    project_queries(0, pl.ds(0, targets))
 
     own_in.wait()
-    for copy in in_copies:
-        copy.wait()
+    for bits in range(1, n_seq):
+        in_copy(bits).wait()
 
     tile = min(256, units)
 
@@ -689,19 +718,36 @@
             for k in range(2):
                 out_copy(bits, j, k).wait_send()
 
-    state = dec_ref[...].astype(jnp.float32)
+    state = [dec_ref[rows_of(part), :].astype(jnp.float32) for part in range(parts)]
+    per_part = n_seq // parts
+    finish = [None] * parts
     for layer in range(layers):
-        if layer > 0:
-            dec_all[layer, m] = state.astype(jnp.bfloat16)
-            plane_gather(dec_all.at[layer], dec_ps.at[layer], dec_pr.at[layer])()
-            normalise(dec_all.at[layer], dec_normed, targets, dec_gain_ref, layer)
-            project_queries(layer)
-        attend()
-        scatter_output(layer)
+        for part in range(parts):
+            if layer > 0:
+                finish[part]()
+                span = rows_of(part)
+                normalise(
+                    dec_next.at[layer - 1, part], dec_normed.at[span], part_rows, dec_gain_ref, layer
+                )
+                project_queries(layer, span)
+            attend(part * per_part, per_part)
+            scatter_output(layer, part)
         if layer + 1 < layers:
             project_memory(layer + 1)
-        state = state + collect_output(layer)
-    out_ref[...] = state.astype(out_ref.dtype)
+        for part in range(parts):
+            state[part] = state[part] + collect_output(layer, part)
+            if layer + 1 < layers:
+                dec_next[layer, part, m] = state[part].astype(jnp.bfloat16)
+                index = 1 + layer * parts + part
+                finish[part] = plane_gather(
+                    dec_next.at[layer, part], dec_ps.at[index], dec_pr.at[index]
+                )
+            else:
+                out_ref[rows_of(part), :] = state[part].astype(out_ref.dtype)
+    for layer in range(layers):
+        for part in range(parts):
+            for bits in range(1, n_mp):
+                att_copy(layer, part, flip(m, bits), m).wait_send()
 
 
 def whole_fast(
@@ -773,7 +819,8 @@
             pltpu.VMEM(w_value.shape, half),
             pltpu.VMEM(w_output.shape, half),
             dma((2 + 2 * n_mp,)),
-            pltpu.VMEM((layers, n_mp, targets, width), half),
+            pltpu.VMEM((n_mp, targets, width), half),
+            pltpu.VMEM((layers, 2, n_mp, targets // 2, width), half),
             pltpu.VMEM((targets, full), half),
             pltpu.VMEM((targets, heads_width), half),
             pltpu.VMEM((slot_total, full), half),
@@ -782,12 +829,12 @@
             pltpu.VMEM((slot_total, heads_width), half),
             pltpu.VMEM((slot_total, heads_width), half),
             pltpu.VMEM((targets, heads_width), half),
-            pltpu.VMEM((layers, n_mp, targets, width), half),
-            pltpu.VMEM((layers, n_mp, targets, width), half),
-            dma((layers, n_mp)),
-            dma((layers, n_mp)),
-            dma((layers, n_mp)),
-            dma((layers, n_mp)),
+            pltpu.VMEM((layers, 2, n_mp, targets // 2, width), half),
+            pltpu.VMEM((layers, 2, n_mp, targets // 2, width), half),
+            dma((2 * layers, n_mp)),
+            dma((2 * layers, n_mp)),
+            dma((layers, 2, n_mp)),
+            dma((layers, 2, n_mp)),
             pltpu.VMEM((n_seq, slot_total // n_seq, rows), half),
             pltpu.VMEM((n_seq, 1, slot_total // n_seq), jnp.float32),
             dma((per_block,)),

time: 258 us -> 253 us (0.981)
  Pallas kernels: 256 us -> 252 us
    pallas_call x1, Pallas kernels: 256 us -> 252 us  [whole_fast(): pl.pallas_call(functools.partial(ffn_kernel, n_seq, n_mp), out_shape=jax....]
where the time goes in v3:
time: 253 us
  Pallas kernels  252 us (100%)
    pallas_call x1, Pallas kernels, whole_fast(): pl.pallas_call(functools.partial(ffn_kernel, n_seq, n_mp), out_shape=jax....  252 us

profile of v3, /device:TPU:0, one launch (start us, length us, event | category | flops | bytes accessed | tf_op | source)
XLA Modules:
  0.0 253.1 jit_solution(10519665731360176011)
XLA Ops:
  0.0 251.6 %shard_map.127 = bf16[256,128]{1,0:T(8,128)(2,1)} custom-call(bf16[256,128]{1,0:T(8,128)(2,1)} %enc_ref.1, f32[1,1024]{1,0:T(1,128)} %bitcast.2, f32[1,1024]{1,0:T(1,128)} %bitcast.3, s32[4,4]{1,0:T(4,128)} %lengths_ref.1, s32[4,4]{1,0:T(4,128)} %table_ref.1, bf16[256,128]{1,0:T(8,128)(2,1)} %dec_ref.1, f32[2,1024]{1,0:T(2,128)} %dec_gain_ref.1, ...), custom_call_target="tpu_custom_call" | custom-call | tf_op jit(solution)/shard_map/pallas_call | solution.py:781
  251.6 1.5 copy.15

commit v4 on v3

--- a/solution.py
+++ b/solution.py
@@ -161,6 +161,26 @@
 
         return finish
 
+    def direct_gather(buf, send_sem, recv_sem):
+        def copy(bits):
+            return pltpu.make_async_remote_copy(
+                src_ref=buf.at[m],
+                dst_ref=buf.at[m],
+                send_sem=send_sem.at[bits],
+                recv_sem=recv_sem.at[bits],
+                device_id=(s, flip(m, bits)),
+                device_id_type=MESH,
+            )
+
+        for bits in range(n_mp - 1, 0, -1):
+            copy(bits).start()
+
+        def finish():
+            for bits in range(1, n_mp):
+                copy(bits).wait()
+
+        return finish
+
     def normalise(buf, dst, count, gain, gain_row):
         step = min(256, count)
 
@@ -274,7 +294,9 @@
             tops = [jnp.max(score, axis=1, keepdims=True) for score in scores]
             powers = [jnp.exp(score - top) for score, top in zip(scores, tops)]
             sums = [jnp.sum(power, axis=1, keepdims=True) for power in powers]
-            weights = [(power / total).astype(jnp.bfloat16) for power, total in zip(powers, sums)]
+            weights = [
+                (power * (1.0 / total)).astype(jnp.bfloat16) for power, total in zip(powers, sums)
+            ]
             for cols, weight in zip(columns, weights):
                 attended[span, cols] = jnp.dot(
                     weight, values[slot_span, cols], preferred_element_type=jnp.float32
@@ -690,20 +712,17 @@
         tree_up(early, 2)
         tree_across(early, 2)
         receive_block(3, far, 1)
+        tree_up(last, 2)
+        tree_across(last, 2)
 
     tree_down(early, 2, enc_b)
     finish_b = plane_gather(enc_b, ag_s.at[1], ag_r.at[1])
-
-    @pl.when(inner == 0)
-    def _():
-        tree_up(last, 2)
-        tree_across(last, 2)
-
+    tree_down(last, 2, enc_c)
+    finish_c = plane_gather(enc_c, ag_s.at[2], ag_r.at[2])
     finish_b()
     absorb(enc_b, early, 2)
     project_part(early * width, 2 * width, False)
-    tree_down(last, 2, enc_c)
-    plane_gather(enc_c, ag_s.at[2], ag_r.at[2])()
+    finish_c()
     absorb(enc_c, last, 2)
     project_last(last * width, 2 * width)
 
@@ -732,16 +751,16 @@
                 project_queries(layer, span)
             attend(part * per_part, per_part)
             scatter_output(layer, part)
-        if layer + 1 < layers:
-            project_memory(layer + 1)
         for part in range(parts):
             state[part] = state[part] + collect_output(layer, part)
             if layer + 1 < layers:
                 dec_next[layer, part, m] = state[part].astype(jnp.bfloat16)
                 index = 1 + layer * parts + part
-                finish[part] = plane_gather(
+                finish[part] = direct_gather(
                     dec_next.at[layer, part], dec_ps.at[index], dec_pr.at[index]
                 )
+                if part == 0:
+                    project_memory(layer + 1)
             else:
                 out_ref[rows_of(part), :] = state[part].astype(out_ref.dtype)
     for layer in range(layers):

time: 253 us -> 250 us (0.988)
  Pallas kernels: 252 us -> 249 us
    pallas_call x1, Pallas kernels: 252 us -> 249 us  [whole_fast(): pl.pallas_call(functools.partial(ffn_kernel, n_seq, n_mp), out_shape=jax....]
where the time goes in v4:
time: 250 us
  Pallas kernels  249 us (100%)
    pallas_call x1, Pallas kernels, whole_fast(): pl.pallas_call(functools.partial(ffn_kernel, n_seq, n_mp), out_shape=jax....  249 us

profile of v4, /device:TPU:0, one launch (start us, length us, event | category | flops | bytes accessed | tf_op | source)
XLA Modules:
  0.0 250.1 jit_solution(15978099777892364517)
XLA Ops:
  0.0 248.6 %shard_map.127 = bf16[256,128]{1,0:T(8,128)(2,1)} custom-call(bf16[256,128]{1,0:T(8,128)(2,1)} %enc_ref.1, f32[1,1024]{1,0:T(1,128)} %bitcast.2, f32[1,1024]{1,0:T(1,128)} %bitcast.3, s32[4,4]{1,0:T(4,128)} %lengths_ref.1, s32[4,4]{1,0:T(4,128)} %table_ref.1, bf16[256,128]{1,0:T(8,128)(2,1)} %dec_ref.1, f32[2,1024]{1,0:T(2,128)} %dec_gain_ref.1, ...), custom_call_target="tpu_custom_call" | custom-call | tf_op jit(solution)/shard_map/pallas_call | solution.py:800
  248.6 1.5 copy.15

commit v5 on v4

--- a/solution.py
+++ b/solution.py
@@ -613,11 +613,11 @@
             for bits in z_order(n_seq):
                 tree_copy(bits, p0, count).start()
 
-    def tree_down(p0, count, enc_buf):
+    def tree_down(p0, count, enc_buf, first=0):
         def combine(own):
             for p in range(p0, p0 + count):
                 total = own[p].astype(jnp.float32) + tree_in[2, p].astype(jnp.float32)
-                enc_buf[m, p - p0] = (total + residual(p)).astype(jnp.bfloat16)
+                enc_buf[m, p - p0 + first] = (total + residual(p)).astype(jnp.bfloat16)
 
         tree_copy(2, p0, count).wait_recv()
 
@@ -712,12 +712,16 @@
         tree_up(early, 2)
         tree_across(early, 2)
         receive_block(3, far, 1)
-        tree_up(last, 2)
-        tree_across(last, 2)
+        tree_copy(0, last, 2).wait_recv()
+        for p in (last + s // 2, last + 1 - s // 2):
+            tree_out[1, p] = (plane_sum(p) + tree_in[0, p].astype(jnp.float32)).astype(jnp.bfloat16)
+            for bits in z_order(n_seq):
+                tree_copy(bits, p, 1).start()
 
     tree_down(early, 2, enc_b)
     finish_b = plane_gather(enc_b, ag_s.at[1], ag_r.at[1])
-    tree_down(last, 2, enc_c)
+    for p in range(last, last + 2):
+        tree_down(p, 1, enc_c, p - last)
     finish_c = plane_gather(enc_c, ag_s.at[2], ag_r.at[2])
     finish_b()
     absorb(enc_b, early, 2)
@@ -731,7 +735,16 @@
             rs_copy(p, flip(m, bits), m).wait_send()
     tree_finish(0, early)
     tree_finish(early, 2)
-    tree_finish(last, 2)
+    @pl.when(inner == 1)
+    def _():
+        tree_copy(0, last, 2).wait_send()
+
+    @pl.when(inner == 0)
+    def _():
+        for p in range(last, last + 2):
+            for bits in z_order(n_seq):
+                tree_copy(bits, p, 1).wait_send()
+
     for bits in range(1, n_seq):
         for j in range(per_block):
             for k in range(2):

time: 250 us -> 249 us (level)
  no operation moved by 1% of the time
where the time goes in v5:
time: 249 us
  Pallas kernels  247 us (99%)
    pallas_call x1, Pallas kernels, whole_fast(): pl.pallas_call(functools.partial(ffn_kernel, n_seq, n_mp), out_shape=jax....  247 us

profile of v5, /device:TPU:0, one launch (start us, length us, event | category | flops | bytes accessed | tf_op | source)
XLA Modules:
  0.0 248.7 jit_solution(1631392863727550354)
XLA Ops:
  0.0 247.2 %shard_map.127 = bf16[256,128]{1,0:T(8,128)(2,1)} custom-call(bf16[256,128]{1,0:T(8,128)(2,1)} %enc_ref.1, f32[1,1024]{1,0:T(1,128)} %bitcast.2, f32[1,1024]{1,0:T(1,128)} %bitcast.3, s32[4,4]{1,0:T(4,128)} %lengths_ref.1, s32[4,4]{1,0:T(4,128)} %table_ref.1, bf16[256,128]{1,0:T(8,128)(2,1)} %dec_ref.1, f32[2,1024]{1,0:T(2,128)} %dec_gain_ref.1, ...), custom_call_target="tpu_custom_call" | custom-call | tf_op jit(solution)/shard_map/pallas_call | solution.py:813
  247.3 1.5 copy.15

commit v6 on v5

--- a/solution.py
+++ b/solution.py
@@ -711,10 +711,17 @@
         receive_block(3, far, 0)
         tree_up(early, 2)
         tree_across(early, 2)
+        tree_out[0, last + s // 2] = plane_sum(last + s // 2).astype(jnp.bfloat16)
         receive_block(3, far, 1)
         tree_copy(0, last, 2).wait_recv()
+        ready = True
         for p in (last + s // 2, last + 1 - s // 2):
-            tree_out[1, p] = (plane_sum(p) + tree_in[0, p].astype(jnp.float32)).astype(jnp.bfloat16)
+            if ready:
+                value = tree_out[0, p].astype(jnp.float32)
+            else:
+                value = plane_sum(p)
+            ready = False
+            tree_out[1, p] = (value + tree_in[0, p].astype(jnp.float32)).astype(jnp.bfloat16)
             for bits in z_order(n_seq):
                 tree_copy(bits, p, 1).start()
 

time: 249 us -> 249 us (level)
  no operation moved by 1% of the time
where the time goes in v6:
time: 249 us
  Pallas kernels  247 us (99%)
    pallas_call x1, Pallas kernels, whole_fast(): pl.pallas_call(functools.partial(ffn_kernel, n_seq, n_mp), out_shape=jax....  247 us

profile of v6, /device:TPU:0, one launch (start us, length us, event | category | flops | bytes accessed | tf_op | source)
XLA Modules:
  0.0 248.7 jit_solution(16176094485198797090)
XLA Ops:
  0.0 247.3 %shard_map.127 = bf16[256,128]{1,0:T(8,128)(2,1)} custom-call(bf16[256,128]{1,0:T(8,128)(2,1)} %enc_ref.1, f32[1,1024]{1,0:T(1,128)} %bitcast.2, f32[1,1024]{1,0:T(1,128)} %bitcast.3, s32[4,4]{1,0:T(4,128)} %lengths_ref.1, s32[4,4]{1,0:T(4,128)} %table_ref.1, bf16[256,128]{1,0:T(8,128)(2,1)} %dec_ref.1, f32[2,1024]{1,0:T(2,128)} %dec_gain_ref.1, ...), custom_call_target="tpu_custom_call" | custom-call | tf_op jit(solution)/shard_map/pallas_call | solution.py:820
  247.3 1.5 copy.15
